TPU v7x, 32 devices: a whole 2x2x4 slice. The times are simulated.
32 devices in a mesh: groups: 1, row: 8 (over z, y), col: 4 (over x, core).
Axes of the slice: x: 2, y: 2, z: 4, core: 2. Of those that a mesh axis runs over, the one named last changes fastest.
Arguments:
- activations: bfloat16 [1024, 16384], P('groups', ('row', 'col')), may hold values from -2.5 to 2.5
- token_ids: int32 [1024], P('groups'), may hold values from 0 to 128255
- initial: float32 [16384, 256], P(('groups', 'row', 'col')), may hold values from -6 to 6
- block_mask: int32 [128, 2], P('groups'), may hold values 0 or 1
Outputs:
- gram: float32 [8, 4, 512, 16384], P('groups', 'col', None, 'row')
- repaired: float32 [16384, 256], P(('groups', 'row', 'col'))
All inputs are finite; a program needn't handle non-finite values.
Results may differ from a plain program's by a relative error of at most 0.0003.
Values may be sent and summed in bfloat16 or wider, within the bound.
No kernel may reach another device: no remote copies, remote signals or barrier semaphores. Data moves between devices by JAX's collectives and lax.ppermute only.
A program may use at most 128 MiB of HBM per device.

v0:
```python
import math
import jax
import jax.numpy as jnp
from jax import lax
from jax.sharding import PartitionSpec as P

D = 16384
ROWS = 1024
BLOCK = 128
ITERS = 2


def shards(activations, token_ids, initial, block_mask):
    matches = (token_ids[:, None] == token_ids[None, :]).astype(jnp.float32)
    weights = 1.0 / jnp.sum(matches, axis=1)
    weighted = (activations.astype(jnp.float32) * weights[:, None]).astype(jnp.bfloat16)
    column_panel = lax.all_gather(activations, "col", axis=1, tiled=True)
    gram_tile = lax.dot_general(
        lax.all_gather(weighted, "row", axis=1, tiled=True),
        column_panel,
        (((0,), (0,)), ((), ())),
        preferred_element_type=jnp.float32,
    ) * (1.0 / ROWS)
    shard_rows = initial.shape[0]
    col_count = lax.axis_size("col")
    first_feature = (lax.axis_index("row") * col_count + lax.axis_index("col")) * shard_rows
    block_index = (first_feature + jnp.arange(shard_rows, dtype=jnp.int32)) // BLOCK
    selector = (
        block_index[:, None] == jnp.arange(block_mask.shape[0], dtype=jnp.int32)[None, :]
    ).astype(jnp.float32)
    mask_rows = jnp.dot(selector, block_mask.astype(jnp.float32), precision=lax.Precision.HIGHEST)
    mask_full = jnp.repeat(mask_rows, BLOCK, axis=1)
    step_size = ROWS / (D + 2.0 * math.sqrt(D * ROWS) + ROWS)
    current = mask_full * initial
    for iteration in range(ITERS):
        change_now = current - initial
        projected = jnp.dot(
            activations.astype(jnp.float32), change_now, precision=lax.Precision.HIGHEST
        )
        totals = lax.psum(projected, ("row", "col"))
        pulled = lax.dot_general(
            weighted.astype(jnp.float32),
            totals,
            (((0,), (0,)), ((), ())),
            precision=lax.Precision.HIGHEST,
        ) * (1.0 / ROWS)
        current = mask_full * (current - step_size * pulled)
    gram_out = gram_tile.reshape(lax.axis_size("row"), 1, shard_rows, gram_tile.shape[1])
    return (gram_out, current)


def solution(mesh):
    in_specs = (
        P("groups", ("row", "col")),
        P("groups"),
        P(("groups", "row", "col"), None),
        P("groups", None),
    )
    out_specs = (P("groups", "col", None, "row"), P(("groups", "row", "col"), None))
    return jax.shard_map(shards, mesh=mesh, in_specs=in_specs, out_specs=out_specs, check_vma=False)
```

profile of v0, /device:TPU:0, one launch (start us, length us, event | category | flops | bytes accessed | tf_op | source)
XLA Modules:
  0.0 426.7 jit_solution(2539099986985370560)
XLA Ops:
  8.0 0.0 copy-start
  8.0 0.0 copy-start.2
  8.0 0.0 all-reduce.3.cloned.1.call-start
  8.1 1.1 fusion.8
  9.2 0.6 broadcast_in_dim.2
  9.8 4.3 %convolution_bitcast_fusion.1 = f32[1024,256]{0,1:T(8,128)} fusion(bf16[1024,512]{1,0:T(8,128)(2,1)} %param.4, f32[512,256]{1,0:T(8,128)} %param.6, f32[64,8,2,128]{3,2,1,0:T(2,128)S(1)} %bitcast.25), kind=kOutput, calls=%fused_computation.4 | convolution fusion | flops 1610874880 | bytes 3145728 | tf_op jit(solution)/shard_map/dot_general | solution.py:37
  14.1 0.0 all-reduce.3.cloned.1.call-update
  14.1 0.0 all-reduce.5.cloned.1.call-start
  14.1 0.0 copy-done.2
  14.1 0.5 convert_reduce_fusion
  14.7 0.0 copy-done
  14.7 0.3 multiply_convert_fusion
  15.0 0.0 copy-start.1
  15.0 132.6 %all-reduce.3.cloned.1.call-done = f32[1024,256]{0,1:T(8,128)} async-done(((f32[1024,256]{0,1:T(8,128)}), f32[1024,256]{0,1:T(8,128)}) %all-reduce.3.cloned.1.call-update) | async-done | bytes 1048592 | tf_op jit(solution)/shard_map/psum | solution.py:40
  147.6 2.6 fusion.1
  150.3 3.9 convolution_bitcast_fusion
  154.1 0.0 all-reduce.5.cloned.1.call-update
  154.2 0.0 all-gather.5.cloned.1.call-start
  154.2 0.5 all-gather.5.cloned.1.call-update
  154.7 0.2 all-gather.3.cloned.1.call-start
  155.0 0.4 all-gather.3.cloned.1.call-update
  155.3 234.5 %all-reduce.5.cloned.1.call-done = f32[1024,256]{0,1:T(8,128)} async-done(((f32[1024,256]{0,1:T(8,128)}), f32[1024,256]{0,1:T(8,128)}) %all-reduce.5.cloned.1.call-update) | async-done | bytes 1048592 | tf_op jit(solution)/shard_map/psum | solution.py:40
  389.9 3.6 fusion.3
  393.5 25.8 %convolution_multiply_fusion = f32[4096,2048]{1,0:T(8,128)} fusion(bf16[1024,4096]{1,0:T(8,128)(2,1)} %all-gather.3.cloned.1.call-done, bf16[1024,2048]{1,0:T(8,128)(2,1)} %all-gather.5.cloned.1.call-done), kind=kOutput, calls=%fused_computation | convolution fusion | flops 17188257792 | bytes 46137344 | tf_op jit(solution)/shard_map/dot_general | solution.py:18
  (5 shorter events, 0.0 us)
Async XLA Ops:
  8.0 6.7 %copy-start = (bf16[1024,512]{1,0:T(8,128)(2,1)S(1)}, bf16[1024,512]{1,0:T(8,128)(2,1)}, u32[]{:S(2)}) copy-start(bf16[1024,512]{1,0:T(8,128)(2,1)} %param.4) | copy-start | bytes 3145732
  8.0 6.1 %copy-start.2 = (s32[1024]{0:T(1024)S(1)}, s32[1024]{0:T(1024)}, u32[]{:S(2)}) copy-start(s32[1024]{0:T(1024)} %param.5) | copy-start | bytes 12292
  8.0 139.6 %all-reduce.3.cloned.1.call-start = ((), (), s32[]{:S(2)}) async-start(), calls=%async_computation.2 | async-start | bytes 2097152 | tf_op jit(solution)/shard_map/psum | solution.py:40
  14.1 375.8 %all-reduce.5.cloned.1.call-start = ((), (), s32[]{:S(2)}) async-start(), calls=%async_computation.3 | async-start | bytes 2097152 | tf_op jit(solution)/shard_map/psum | solution.py:40
  15.0 139.7 %copy-start.1 = (bf16[1024,512]{1,0:T(8,128)(2,1)}, bf16[1024,512]{1,0:T(8,128)(2,1)S(1)}, u32[]{:S(2)}) copy-start(bf16[1024,512]{1,0:T(8,128)(2,1)S(1)} %multiply_convert_fusion) | copy-start | bytes 3145732
  154.2 239.3 %all-gather.5.cloned.1.call-start = ((), (), s32[]{:S(2)}) async-start(), calls=%async_computation.1 | async-start | bytes 5242880 | tf_op jit(solution)/shard_map/all_gather | solution.py:17
  154.7 238.7 %all-gather.3.cloned.1.call-start = ((), (), s32[]{:S(2)}) async-start(), calls=%async_computation | async-start | bytes 9437184 | tf_op jit(solution)/shard_map/all_gather | solution.py:19
Sparse Core Ops, SparseCore 0:
  14.2 133.3 all-reduce.2
  154.3 235.5 all-reduce.4
Sparse Core Ops, SparseCore 1:
  156.2 33.8 all-gather.4
  192.5 125.3 all-gather.2
where the time goes:
time: 427 us
  waiting for transfers between devices  368 us (86%)
  matrix products  41.3 us (10%)
  between operations  15.6 us (4%)
    psum x2, waiting for transfers between devices, shards(): totals = lax.psum(projected, ('row', 'col'))  367 us
    dot_general x1, matrix products, shards(): lax.dot_general(lax.all_gather(weighted, 'row', axis=1, tiled=True), colu...  25.8 us
  transfers between devices with their start and end apart: 4, of which 2 were waited for; matrix products, arithmetic and copies ran while one was open for 1% of the time, Pallas kernels for 0%

commit v1 on v0

--- a/solution.py
+++ b/solution.py
@@ -37,7 +37,7 @@
         projected = jnp.dot(
             activations.astype(jnp.float32), change_now, precision=lax.Precision.HIGHEST
         )
-        totals = lax.psum(projected, ("row", "col"))
+        totals = lax.psum(lax.psum(projected, "row"), "col")
         pulled = lax.dot_general(
             weighted.astype(jnp.float32),
             totals,

time: 427 us -> 453 us (1.061)
  waiting for transfers between devices: 368 us -> 395 us
    psum x2 -> x4, waiting for transfers between devices: 367 us -> 234 us  [shards(): totals = lax.psum(lax.psum(projected, 'row'), 'col')]
    all_gather x1, waiting for transfers between devices: 0.01 us -> 127 us  [shards(): lax.all_gather(weighted, 'row', axis=1, tiled=True)]
    all_gather x1, waiting for transfers between devices: 0.01 us -> 32.8 us  [shards(): column_panel = lax.all_gather(activations, 'col', axis=1, tiled=True)]
  transfers between devices with their start and end apart: 4 -> 6, of which waited for: 2 -> 6; matrix products, arithmetic and copies ran while one was open for 1% -> 1% of each run, Pallas kernels for 0% -> 0%
where the time goes in v1:
time: 453 us
  waiting for transfers between devices  395 us (87%)
  matrix products  41.2 us (9%)
  between operations  14.2 us (3%)
    psum x4, waiting for transfers between devices, shards(): totals = lax.psum(lax.psum(projected, 'row'), 'col')  234 us
    all_gather x1, waiting for transfers between devices, shards(): lax.all_gather(weighted, 'row', axis=1, tiled=True)  127 us
    all_gather x1, waiting for transfers between devices, shards(): column_panel = lax.all_gather(activations, 'col', axis=1, tiled=True)  32.8 us
    dot_general x1, matrix products, shards(): lax.dot_general(lax.all_gather(weighted, 'row', axis=1, tiled=True), colu...  25.8 us
  transfers between devices with their start and end apart: 6, of which 6 were waited for; matrix products, arithmetic and copies ran while one was open for 1% of the time, Pallas kernels for 0%

profile of v1, /device:TPU:0, one launch (start us, length us, event | category | flops | bytes accessed | tf_op | source)
XLA Modules:
  0.0 452.7 jit_solution(12107221585294015672)
XLA Ops:
  7.2 0.0 all-reduce.5.cloned.1.call-start
  7.3 1.1 fusion.8
  8.3 0.6 broadcast_in_dim.2
  8.9 4.2 convolution_bitcast_fusion.1
  13.2 0.0 all-reduce.5.cloned.1.call-update
  13.2 0.0 all-reduce.7.cloned.1.call-start
  13.2 81.1 %all-reduce.5.cloned.1.call-done = f32[1024,256]{0,1:T(8,128)} async-done(((f32[1024,256]{0,1:T(8,128)}), f32[1024,256]{0,1:T(8,128)}) %all-reduce.5.cloned.1.call-update) | async-done | bytes 1048592 | tf_op jit(solution)/shard_map/psum | solution.py:40
  94.4 0.0 all-reduce.9.cloned.1.call-start
  94.5 0.5 convert_reduce_fusion
  95.0 0.3 multiply_convert_fusion
  95.3 37.3 %all-reduce.7.cloned.1.call-done = f32[1024,256]{0,1:T(8,128)} async-done(((f32[1024,256]{0,1:T(8,128)}), f32[1024,256]{0,1:T(8,128)}) %all-reduce.7.cloned.1.call-update) | async-done | bytes 1048592 | tf_op jit(solution)/shard_map/psum | solution.py:40
  132.7 2.6 fusion.1
  135.3 3.9 convolution_bitcast_fusion
  139.2 0.0 all-reduce.11.cloned.1.call-start
  139.3 78.9 %all-reduce.9.cloned.1.call-done = f32[1024,256]{0,1:T(8,128)} async-done(((f32[1024,256]{0,1:T(8,128)}), f32[1024,256]{0,1:T(8,128)}) %all-reduce.9.cloned.1.call-update) | async-done | bytes 1048592 | tf_op jit(solution)/shard_map/psum | solution.py:40
  218.2 0.0 all-gather.5.cloned.1.call-start
  218.2 0.5 all-gather.5.cloned.1.call-update
  218.8 0.2 all-gather.3.cloned.1.call-start
  219.0 0.3 all-gather.3.cloned.1.call-update
  219.3 36.9 %all-reduce.11.cloned.1.call-done = f32[1024,256]{0,1:T(8,128)} async-done(((f32[1024,256]{0,1:T(8,128)}), f32[1024,256]{0,1:T(8,128)}) %all-reduce.11.cloned.1.call-update) | async-done | bytes 1048592 | tf_op jit(solution)/shard_map/psum | solution.py:40
  256.3 3.6 fusion.3
  259.9 32.8 %all-gather.5.cloned.1.call-done = bf16[1024,2048]{1,0:T(8,128)(2,1)} async-done(((bf16[1024,512]{1,0:T(8,128)(2,1)}), bf16[1024,2048]{1,0:T(8,128)(2,1)}) %all-gather.5.cloned.1.call-update) | async-done | bytes 4194320 | tf_op jit(solution)/shard_map/all_gather | solution.py:17
  292.7 127.4 %all-gather.3.cloned.1.call-done = bf16[1024,4096]{1,0:T(8,128)(2,1)} async-done(((bf16[1024,512]{1,0:T(8,128)(2,1)}), bf16[1024,4096]{1,0:T(8,128)(2,1)}) %all-gather.3.cloned.1.call-update) | async-done | bytes 8388624 | tf_op jit(solution)/shard_map/all_gather | solution.py:19
  420.1 25.8 %convolution_multiply_fusion = f32[4096,2048]{1,0:T(8,128)} fusion(bf16[1024,4096]{1,0:T(8,128)(2,1)} %all-gather.3.cloned.1.call-done, bf16[1024,2048]{1,0:T(8,128)(2,1)} %all-gather.5.cloned.1.call-done), kind=kOutput, calls=%fused_computation | convolution fusion | flops 17188257792 | bytes 46137344 | tf_op jit(solution)/shard_map/dot_general | solution.py:18
  (11 shorter events, 0.1 us)
Async XLA Ops:
  7.2 87.8 %copy-start = (bf16[1024,512]{1,0:T(8,128)(2,1)S(1)}, bf16[1024,512]{1,0:T(8,128)(2,1)}, u32[]{:S(2)}) copy-start(bf16[1024,512]{1,0:T(8,128)(2,1)} %param.4) | copy-start | bytes 3145732
  7.2 87.3 %copy-start.2 = (s32[1024]{0:T(1024)S(1)}, s32[1024]{0:T(1024)}, u32[]{:S(2)}) copy-start(s32[1024]{0:T(1024)} %param.5) | copy-start | bytes 12292
  7.2 87.2 %all-reduce.5.cloned.1.call-start = ((), (), s32[]{:S(2)}) async-start(), calls=%async_computation.2 | async-start | bytes 2097152 | tf_op jit(solution)/shard_map/psum | solution.py:40
  13.2 119.5 %all-reduce.7.cloned.1.call-start = ((), (), s32[]{:S(2)}) async-start(), calls=%async_computation.3 | async-start | bytes 2097152 | tf_op jit(solution)/shard_map/psum | solution.py:40
  94.4 123.7 %all-reduce.9.cloned.1.call-start = ((), (), s32[]{:S(2)}) async-start(), calls=%async_computation.4 | async-start | bytes 2097152 | tf_op jit(solution)/shard_map/psum | solution.py:40
  95.3 122.8 %copy-start.1 = (bf16[1024,512]{1,0:T(8,128)(2,1)}, bf16[1024,512]{1,0:T(8,128)(2,1)S(1)}, u32[]{:S(2)}) copy-start(bf16[1024,512]{1,0:T(8,128)(2,1)S(1)} %multiply_convert_fusion) | copy-start | bytes 3145732
  139.2 117.1 %all-reduce.11.cloned.1.call-start = ((), (), s32[]{:S(2)}) async-start(), calls=%async_computation.5 | async-start | bytes 2097152 | tf_op jit(solution)/shard_map/psum | solution.py:40
  218.2 74.5 %all-gather.5.cloned.1.call-start = ((), (), s32[]{:S(2)}) async-start(), calls=%async_computation.1 | async-start | bytes 5242880 | tf_op jit(solution)/shard_map/all_gather | solution.py:17
  218.8 201.3 %all-gather.3.cloned.1.call-start = ((), (), s32[]{:S(2)}) async-start(), calls=%async_computation | async-start | bytes 9437184 | tf_op jit(solution)/shard_map/all_gather | solution.py:19
Sparse Core Ops, SparseCore 0:
  13.3 81.0 all-reduce.4
  96.7 35.8 all-reduce.6
  139.3 78.7 all-reduce.8
  220.4 35.8 all-reduce.10
  257.7 34.9 all-gather.4
  295.1 124.9 all-gather.2
